TPU v7x, 32 devices: a whole 2x2x4 slice. The times are simulated.
32 devices in a mesh: freq: 4 (over z), tm: 4 (over x, core), grp: 2 (over y).
Axes of the slice: x: 2, y: 2, z: 4, core: 2. Of those that a mesh axis runs over, the one named last changes fastest.
Arguments:
- voltages: bfloat16 [4, 2, 1024, 4096], P(None, None, ('freq', 'grp'), 'tm'), may hold values from -6 to 6
- prior_gains: float32 [4, 2, 1024], P('freq'), may hold values from -4.2 to 4.2
- station_flags: int32 [512], replicated, may hold values 0 or 1
- ingest_map: int32 [512], replicated, may hold values from 0 to 511, each once
- station_coords: float32 [2, 512], replicated, may hold values from -40 to 40
- pointing: int32 [2, 256], replicated, may hold values from 0 to 63
- corr_channels: int32 [4], replicated, may hold values from 0 to 3, each once
- beam_channels: int32 [4], replicated, may hold values from 0 to 3, each once
Outputs:
- visibilities: float32 [4, 2, 1024, 1024], P('freq', None, 'grp', 'tm')
- solved_gains: float32 [4, 2, 1024], P('freq')
- tied_beams: bfloat16 [4, 2, 2, 256, 4096], P('freq', None, None, 'grp', 'tm')
Inputs may be any that keep to these rules, and one draw needn't show every extreme that they name: `ingest_map`: each station appears in exactly one ingest slot. `corr_channels`: each channel is handled by exactly one correlator slot. `beam_channels`: each channel is handled by exactly one beamformer slot.
All inputs are finite; a program needn't handle non-finite values.
Results may differ from a plain program's by a relative error of at most 0.0049.
Values may be sent and summed in bfloat16 or wider, within the bound.
A program may use at most 64 MiB of HBM per device.

v0:
```python
import math

import jax
import jax.numpy as jnp
from jax import lax
from jax.sharding import PartitionSpec as P

S = 512
ITERS = 4


grid_cells = 64.0


def weights_for(gains_sel, ratio, pointing_part, slot_coords):
    east_dir = (pointing_part[0].astype(jnp.float32) + 0.5) / grid_cells - 0.5
    north_dir = (pointing_part[1].astype(jnp.float32) + 0.5) / grid_cells - 0.5
    phase = (
        2.0
        * math.pi
        * ratio
        * (
            east_dir[:, None] * slot_coords[0][None, :]
            + north_dir[:, None] * slot_coords[1][None, :]
        )
    )
    cosine = jnp.cos(phase)
    sine = jnp.sin(phase)
    gain_real = gains_sel[0].reshape(2, S)
    gain_imag = gains_sel[1].reshape(2, S)
    denom = jnp.maximum(gain_real * gain_real + gain_imag * gain_imag, 0.5)
    along_real = gain_real / denom
    along_imag = gain_imag / denom
    factor = 1.0 / math.sqrt(S)
    w_real = (cosine[None] * along_real[:, None, :] - sine[None] * along_imag[:, None, :]) * factor
    w_imag = -(cosine[None] * along_imag[:, None, :] + sine[None] * along_real[:, None, :]) * factor
    upper = jnp.stack([w_real, -w_imag], axis=2)
    lower = jnp.stack([w_imag, w_real], axis=2)
    return jnp.stack([upper, lower], axis=1).astype(jnp.bfloat16)


def body(
    voltages,
    prior_gains,
    station_flags,
    ingest_map,
    station_coords,
    pointing,
    corr_channels,
    beam_channels,
):
    highest = lax.Precision.HIGHEST
    n_freq = lax.axis_size("freq")
    n_time = lax.axis_size("tm")
    n_group = lax.axis_size("grp")
    freq_index = lax.axis_index("freq")
    time_index = lax.axis_index("tm")
    group_index = lax.axis_index("grp")
    channels_all = voltages.shape[0]
    per_device = channels_all // n_freq
    per_input = voltages.shape[2]
    samples = voltages.shape[3]
    inputs_all = 2 * S
    corr_source = jnp.take(voltages, corr_channels, axis=0)
    beam_source = jnp.take(voltages, beam_channels, axis=0)
    corr_half, beam_half = (
        lax.all_to_all(corr_source, "freq", split_axis=0, concat_axis=2, tiled=True),
        lax.all_to_all(beam_source, "freq", split_axis=0, concat_axis=2, tiled=True),
    )
    split_shape = (per_device, 2, n_freq, per_input, samples)
    corr_pair, beam_pair = (
        lax.all_gather(corr_half.reshape(split_shape), "grp", axis=3, tiled=True),
        lax.all_gather(beam_half.reshape(split_shape), "grp", axis=3, tiled=True),
    )
    full_shape = (per_device, 2, inputs_all, samples)
    corr_volts = corr_pair.reshape(full_shape)
    beam_volts = beam_pair.reshape(full_shape)
    slot_keep = 1 - jnp.take(station_flags, ingest_map)
    keep = jnp.concatenate([slot_keep, slot_keep]).astype(jnp.bfloat16)
    corr_volts = corr_volts * keep[None, None, :, None]
    beam_volts = beam_volts * keep[None, None, :, None]
    rows = inputs_all // n_group
    row_start = group_index * rows
    mine = lax.dynamic_slice_in_dim(corr_volts, row_start, rows, 2)
    left = jnp.stack([mine, jnp.stack([mine[:, 1], -mine[:, 0]], axis=1)], axis=1)
    partial_value = jnp.einsum(
        "corit,crjt->coij", left, corr_volts, preferred_element_type=jnp.float32
    )
    partial_value = partial_value * (1.0 / (samples * n_time))
    columns = inputs_all // n_time
    vis_block = lax.psum_scatter(partial_value, "tm", scatter_dimension=3, tiled=True)
    gains = prior_gains
    for iteration in range(ITERS):
        power = jnp.sum(gains * gains, axis=(1, 2)) + 1e-06
        along = lax.dynamic_slice_in_dim(gains, time_index * columns, columns, 2)
        real_real = jnp.einsum("cij,cj->ci", vis_block[:, 0], along[:, 0], precision=highest)
        imag_imag = jnp.einsum("cij,cj->ci", vis_block[:, 1], along[:, 1], precision=highest)
        real_imag = jnp.einsum("cij,cj->ci", vis_block[:, 0], along[:, 1], precision=highest)
        imag_real = jnp.einsum("cij,cj->ci", vis_block[:, 1], along[:, 0], precision=highest)
        update = jnp.stack([real_real - imag_imag, imag_real + real_imag], axis=1)
        update = lax.psum(update, "tm")
        own_rows = lax.dynamic_slice_in_dim(gains, row_start, rows, 2)
        fresh = 0.5 * (own_rows + inputs_all * update / power[:, None, None])
        gains = lax.all_gather(fresh, "grp", axis=2, tiled=True)
    all_gains = lax.all_gather(gains, "freq", axis=0, tiled=True)
    my_beam = lax.dynamic_slice_in_dim(beam_channels, freq_index * per_device, per_device, 0)
    onehot = (corr_channels[None, :] == my_beam[:, None]).astype(jnp.float32)
    selected = jnp.einsum("ck,kri->cri", onehot, all_gains, precision=highest)
    ratio = 0.875 + 0.25 * (my_beam.astype(jnp.float32) + 0.5) / channels_all
    beams_mine = pointing.shape[1] // n_group
    pointing_part = lax.dynamic_slice_in_dim(pointing, group_index * beams_mine, beams_mine, 1)
    slot_coords = jnp.take(station_coords, ingest_map, axis=1)
    weights = jax.vmap(weights_for, in_axes=(0, 0, None, None))(
        selected, ratio, pointing_part, slot_coords
    )
    block = beam_volts.reshape(per_device, 2, 2, S, samples)
    beams = jnp.einsum("cpobrq,crpqt->cpobt", weights, block, preferred_element_type=jnp.float32)
    return (vis_block, gains, beams.astype(jnp.bfloat16))


def solution(mesh):
    return jax.shard_map(
        body,
        mesh=mesh,
        in_specs=(
            P(None, None, ("freq", "grp"), "tm"),
            P("freq", None, None),
            P(),
            P(),
            P(),
            P(),
            P(),
            P(),
        ),
        out_specs=(
            P("freq", None, "grp", "tm"),
            P("freq", None, None),
            P("freq", None, None, "grp", "tm"),
        ),
        check_vma=False,
    )
```

profile of v0, /device:TPU:0, one launch (start us, length us, event | category | flops | bytes accessed | tf_op | source)
XLA Modules:
  0.0 313.8 jit_solution(3851320219780948037)
XLA Ops:
  7.2 0.8 compare_select_fusion.1
  8.0 0.7 compare_and_fusion
  8.8 2.0 gather_fusion.2
  10.8 1.9 broadcast_select_fusion.1
  12.7 54.4 %all_to_all.30 = bf16[4,2,128,1024]{3,2,1,0:T(8,128)(2,1)} all-to-all(bf16[4,2,128,1024]{3,2,1,0:T(8,128)(2,1)S(1)} %broadcast_select_fusion.1), channel_id=1, replica_groups=mesh['freq'=4,'tm'=4,'grp'=2] {'freq'}, dimensions={0} | all-to-all | bytes 4194304 | tf_op jit(solution)/shard_map/all_to_all | solution.py:67
  67.2 2.0 gather_fusion.3
  69.2 1.9 broadcast_select_fusion
  71.1 50.7 %all_to_all.31 = bf16[4,2,128,1024]{3,2,1,0:T(8,128)(2,1)} all-to-all(bf16[4,2,128,1024]{3,2,1,0:T(8,128)(2,1)S(1)} %broadcast_select_fusion), channel_id=1, replica_groups=mesh['freq'=4,'tm'=4,'grp'=2] {'freq'}, dimensions={0} | all-to-all | bytes 4194304 | tf_op jit(solution)/shard_map/all_to_all | solution.py:68
  121.8 0.6 copy-done.5
  122.5 3.5 %gather_fusion = s32[512]{0:T(512)S(1)} fusion(s32[512]{0:T(512)S(1)} %copy-done.1, s32[1024]{0:T(1024)S(1)} %pad_clamp_fusion.1), kind=kCustom, calls=%fused_computation.2 | custom fusion | bytes 6144 | tf_op jit(solution)/shard_map/jit(_take)/gather | solution.py:78
  126.1 2.5 broadcast_multiply_fusion
  129.1 1.8 copy-done.3
  132.6 6.1 %fusion.5 = f32[1,2,512,1024]{3,2,1,0:T(8,128)} fusion(bf16[2,1024,1024,1]{2,1,0,3:T(8,128)(2,1)S(1)} %bitcast.171, bf16[1,1,2,512,1024]{4,3,2,1,0:T(8,128)(2,1)S(1)} %maximum_bitcast_fusion.4, bf16[1,1,2,512,1024]{4,3,2,1,0:T(8,128)(2,1)S(1)} %fusion.76), kind=kOutput, calls=%fused_computation.11 | convolution fusion | flops 4298113024 | bytes 12582912 | tf_op jit(solution)/shard_map/corit,crjt->coij/dot_general | solution.py:86
  138.8 0.6 copy-done.8
  139.4 0.6 dynamic_slice.42
  140.1 1.0 gather_fusion.1
  141.8 0.6 multiply_reduce_fusion.3
  143.5 1.8 fusion.32
  145.3 36.2 %all-gather.5.cloned.1.call-done = bf16[1,2,4,256,1024]{4,3,1,2,0:T(8,128)(2,1)} async-done(((bf16[1,2,4,128,1024]{4,3,1,2,0:T(8,128)(2,1)}), bf16[1,2,4,256,1024]{4,3,1,2,0:T(8,128)(2,1)}) %all-gather.5.cloned.1.call-update) | async-done | bytes 4194320 | tf_op jit(solution)/shard_map/all_gather | solution.py:73
  181.6 4.6 %copy.27 = bf16[1,2,4,256,1024]{4,3,2,1,0:T(8,128)(2,1)} copy(bf16[1,2,4,256,1024]{4,3,1,2,0:T(8,128)(2,1)} %all-gather.5.cloned.1.call-done) | data formatting | bytes 8388608 | tf_op jit(solution)/shard_map/all_gather | solution.py:73
  186.2 42.9 %reduce-scatter.2.cloned.1.call-done = f32[1,2,512,256]{3,2,1,0:T(8,128)} async-done(((f32[1,2,512,1024]{3,2,1,0:T(8,128)}), f32[1,2,512,256]{3,2,1,0:T(8,128)}) %reduce-scatter.2.cloned.1.call-update) | async-done | bytes 1048592 | tf_op jit(solution)/shard_map/reduce_scatter | solution.py:91
  229.1 1.7 fusion.29
  230.8 1.6 fusion.21
  232.4 1.6 fusion.22
  234.0 1.6 fusion.30
  235.6 5.8 %psum.28 = f32[1,2,512]{2,1,0:T(2,128)S(1)} all-reduce(f32[1,2,512]{2,1,0:T(2,128)S(1)} %pad_maximum_fusion), channel_id=1, replica_groups=mesh['freq'=4,'tm'=4,'grp'=2] {'tm'}, use_global_device_ids=true, to_apply=%region_1.3 | all-reduce | flops 1024 | bytes 8192 | tf_op jit(solution)/shard_map/psum | solution.py:101
  241.4 4.4 %all_gather.22 = f32[1,2,1024]{2,1,0:T(2,128)S(1)} all-gather(f32[1,2,512]{2,1,0:T(2,128)S(1)} %fusion.38), channel_id=1, replica_groups=mesh['freq'=4,'tm'=4,'grp'=2] {'grp'}, dimensions={2}, use_global_device_ids=true | all-gather | bytes 12288 | tf_op jit(solution)/shard_map/all_gather | solution.py:104
  245.8 0.6 multiply_reduce_fusion.2
  246.9 0.6 fusion.19
  247.5 0.6 fusion.20
  248.0 0.6 fusion.28
  248.6 5.7 %psum.29 = f32[1,2,512]{2,1,0:T(2,128)S(1)} all-reduce(f32[1,2,512]{2,1,0:T(2,128)S(1)} %pad_maximum_fusion.1), channel_id=1, replica_groups=mesh['freq'=4,'tm'=4,'grp'=2] {'tm'}, use_global_device_ids=true, to_apply=%region_3.5 | all-reduce | flops 1024 | bytes 8192 | tf_op jit(solution)/shard_map/psum | solution.py:101
  255.0 4.5 %all_gather.23 = f32[1,2,1024]{2,1,0:T(2,128)S(1)} all-gather(f32[1,2,512]{2,1,0:T(2,128)S(1)} %fusion.39), channel_id=1, replica_groups=mesh['freq'=4,'tm'=4,'grp'=2] {'grp'}, dimensions={2}, use_global_device_ids=true | all-gather | bytes 12288 | tf_op jit(solution)/shard_map/all_gather | solution.py:104
  259.5 0.6 multiply_reduce_fusion.1
  260.6 0.6 fusion.17
  261.8 0.6 fusion.26
  262.4 5.7 %psum.30 = f32[1,2,512]{2,1,0:T(2,128)S(1)} all-reduce(f32[1,2,512]{2,1,0:T(2,128)S(1)} %pad_maximum_fusion.2), channel_id=1, replica_groups=mesh['freq'=4,'tm'=4,'grp'=2] {'tm'}, use_global_device_ids=true, to_apply=%region_5.7 | all-reduce | flops 1024 | bytes 8192 | tf_op jit(solution)/shard_map/psum | solution.py:101
  268.7 4.4 %all_gather.24 = f32[1,2,1024]{2,1,0:T(2,128)S(1)} all-gather(f32[1,2,512]{2,1,0:T(2,128)S(1)} %fusion.40), channel_id=1, replica_groups=mesh['freq'=4,'tm'=4,'grp'=2] {'grp'}, dimensions={2}, use_global_device_ids=true | all-gather | bytes 12288 | tf_op jit(solution)/shard_map/all_gather | solution.py:104
  273.1 0.6 multiply_reduce_fusion
  274.2 0.6 fusion.15
  275.3 0.6 fusion.24
  275.9 5.7 %psum.31 = f32[1,2,512]{2,1,0:T(2,128)S(1)} all-reduce(f32[1,2,512]{2,1,0:T(2,128)S(1)} %pad_maximum_fusion.3), channel_id=1, replica_groups=mesh['freq'=4,'tm'=4,'grp'=2] {'tm'}, use_global_device_ids=true, to_apply=%region_7.9 | all-reduce | flops 1024 | bytes 8192 | tf_op jit(solution)/shard_map/psum | solution.py:101
  282.3 4.4 %all_gather.25 = f32[1,2,1024]{2,1,0:T(2,128)S(1)} all-gather(f32[1,2,512]{2,1,0:T(2,128)S(1)} %fusion.41), channel_id=1, replica_groups=mesh['freq'=4,'tm'=4,'grp'=2] {'grp'}, dimensions={2}, use_global_device_ids=true | all-gather | bytes 12288 | tf_op jit(solution)/shard_map/all_gather | solution.py:104
  286.6 13.4 %all_gather.26 = f32[4,2,1024]{2,1,0:T(2,128)S(1)} all-gather(f32[1,2,1024]{2,1,0:T(2,128)S(1)} %all_gather.25), channel_id=1, replica_groups=mesh['freq'=4,'tm'=4,'grp'=2] {'freq'}, dimensions={0}, use_global_device_ids=true | all-gather | bytes 40960 | tf_op jit(solution)/shard_map/all_gather | solution.py:105
  300.0 0.8 fusion.33
  300.9 1.1 negate_convert_fusion
  302.1 4.6 %fusion.8 = bf16[1,2,2,128,1024]{4,3,2,1,0:T(8,128)(2,1)} fusion(bf16[2,1,128,2,512]{4,2,3,1,0:T(8,128)(2,1)S(1)} %get-tuple-element.17, bf16[2,1,128,2,512]{4,2,3,1,0:T(8,128)(2,1)S(1)} %get-tuple-element.16, bf16[2,2,512,1024]{3,2,1,0:T(8,128)(2,1)} %bitcast.170, bf16[2,512]{1,0:T(2,128)(2,1)S(1)} %convert_element_type.50), kind=kOutput, calls=%fused_computation.19 | convolution fusion | flops 1076887552 | bytes 6293504 | tf_op jit(solution)/shard_map/cpobrq,crpqt->cpobt/dot_general | solution.py:117
  306.6 0.6 copy.47
  (71 shorter events, 6.1 us)
Async XLA Ops:
  7.2 1.6 copy-start
  7.2 118.9 %all-gather.3.cloned.1.call-start = ((), (), s32[]{:S(2)}) async-start(), calls=%async_computation.3 | async-start | bytes 6291456 | tf_op jit(solution)/shard_map/all_gather | solution.py:72
  67.2 114.4 %all-gather.5.cloned.1.call-start = ((), (), s32[]{:S(2)}) async-start(), calls=%async_computation.5 | async-start | bytes 6291456 | tf_op jit(solution)/shard_map/all_gather | solution.py:73
  121.8 0.7 copy-start.5
  121.8 0.7 copy-start.1
  121.8 107.3 %reduce-scatter.2.cloned.1.call-start = ((), (), s32[]{:S(2)}) async-start(), calls=%async_computation.4 | async-start | bytes 5242880 | tf_op jit(solution)/shard_map/reduce_scatter | solution.py:91
  128.7 2.3 copy-start.3
  138.7 0.7 copy-start.8
  138.7 1.3 copy-start.7
  138.7 3.1 copy-start.4
  138.7 4.3 %copy-start.9 = (s32[2,256]{1,0:T(2,128)S(1)}, s32[2,256]{1,0:T(2,128)}, u32[]{:S(2)}) copy-start(s32[2,256]{1,0:T(2,128)} %param.15) | copy-start | bytes 6148
  229.1 17.3 %copy-start.2 = (f32[1,2,512,256]{3,2,1,0:T(8,128)S(1)}, f32[1,2,512,256]{3,2,1,0:T(8,128)}, u32[]{:S(2)}) copy-start(f32[1,2,512,256]{3,2,1,0:T(8,128)} %reduce-scatter.2.cloned.1.call-done) | copy-start | bytes 3145732
  260.1 39.9 %copy-start.6 = (s32[4]{0:T(128)S(1)}, s32[4]{0:T(128)}, u32[]{:S(2)}) copy-start(s32[4]{0:T(128)} %param.16) | copy-start | bytes 52
Sparse Core Ops, SparseCore 0:
  67.3 55.9 all-gather.2
  124.8 56.7 all-gather.4
  184.7 44.3 reduce-scatter.1
where the time goes:
time: 315 us; the launch traced here: 314 us
  blocking collectives  159 us (50%)
  waiting for transfers between devices  79.2 us (25%)
  matrix products  24.5 us (8%)
  local copies, waits for them, and re-layouts  19 us (6%)
  between operations  17.3 us (5%)
  other arithmetic  14.7 us (5%)
    all_to_all x1, blocking collectives, body(): lax.all_to_all(corr_source, 'freq', split_axis=0, concat_axis=2, tiled=True)  54.4 us
    all_to_all x1, blocking collectives, body(): lax.all_to_all(beam_source, 'freq', split_axis=0, concat_axis=2, tiled=True)  50.7 us
    reduce_scatter x1, waiting for transfers between devices, body(): lax.psum_scatter(partial_value, 'tm', scatter_dimension=3, tiled=True)  42.9 us
    all_gather x1, waiting for transfers between devices, body(): lax.all_gather(beam_half.reshape(split_shape), 'grp', axis=3, tiled=True)  36.2 us
    psum x4, blocking collectives, body(): update = lax.psum(update, 'tm')  22.8 us
    all_gather x4, blocking collectives, body(): gains = lax.all_gather(fresh, 'grp', axis=2, tiled=True)  17.6 us
    all_gather x1, blocking collectives, body(): all_gains = lax.all_gather(gains, 'freq', axis=0, tiled=True)  13.4 us
  transfers between devices with their start and end apart: 3, of which 2 were waited for; matrix products, arithmetic and copies ran while one was open for 9% of the time, Pallas kernels for 0%

commit v1 on v0

v1 whole, which is shorter than its diff:
```python
import functools
import math

import jax
import jax.numpy as jnp
from jax import lax
from jax.experimental import pallas as pl
from jax.experimental.pallas import tpu as pltpu
from jax.sharding import PartitionSpec as P

ITERS = 4
LANES = 128
grid_cells = 64.0
MESH = pl.DeviceIdType.MESH


def partner(index, mask, count):
    result, bit = 0, 1
    while bit < count:
        digit = (index // bit) % 2
        result = result + bit * ((1 - digit) if mask & bit else digit)
        bit *= 2
    return result


def nt_dot(a, b):
    return lax.dot_general(a, b, (((1,), (1,)), ((), ())), preferred_element_type=jnp.float32)


def kernel(
    nf,
    nt,
    ng,
    chunks,
    src_c,
    src_b,
    prior,
    onehot,
    cosine,
    sine,
    vis_out,
    gains_out,
    beams_out,
    corr,
    beam,
    gram,
    stage,
    landed,
    updates,
    z,
    gains,
    zs,
    zr,
    ys,
    yr,
    own_sem,
    vs,
    vr,
    us,
    ur,
    gs,
    gr,
):
    f = lax.axis_index("freq")
    t = lax.axis_index("tm")
    g = lax.axis_index("grp")
    _, _, per_input, samples = src_c.shape
    inputs = nf * ng * per_input
    rows = inputs // ng
    cols = inputs // nt
    half = inputs // 2
    offsets = [(dt, dg) for dg in range(ng) for dt in range(nt) if (dt, dg) != (0, 0)]
    masks = list(range(nf - 1, 0, -1))
    peers = {k: partner(f, k, nf) for k in range(nf)}

    def group(dt, dg):
        return {"freq": f, "tm": (t + dt) % nt, "grp": (g + dg) % ng}

    def along_freq(k):
        return {"freq": peers[k], "tm": t, "grp": g}

    barrier = pltpu.get_barrier_semaphore()
    for k in masks:
        pl.semaphore_signal(barrier, inc=1, device_id=along_freq(k), device_id_type=MESH)
    for dt, dg in offsets:
        pl.semaphore_signal(barrier, inc=1, device_id=group(dt, dg), device_id_type=MESH)
    pl.semaphore_wait(barrier, len(masks) + len(offsets))

    sources = (src_c, src_b)
    wholes = (corr, beam)

    def place(whole, owner, chunk):
        part, first, count = chunk
        start = pl.multiple_of((owner * ng + g) * per_input + first, count)
        return whole.at[part, pl.ds(start, count), :]

    def z_copy(which, k, ci):
        part, first, count = chunks[ci]
        return pltpu.make_async_remote_copy(
            src_ref=sources[which].at[peers[k], part, pl.ds(first, count), :],
            dst_ref=place(wholes[which], f, chunks[ci]),
            send_sem=zs.at[which, k - 1, ci],
            recv_sem=zr.at[which, k - 1, ci],
            device_id=along_freq(k),
            device_id_type=MESH,
        )

    def y_copy(which, k, ci, dg):
        part, first, count = chunks[ci]
        spot = place(wholes[which], peers[k], chunks[ci])
        origin = sources[which].at[f, part, pl.ds(first, count), :] if k == 0 else spot
        return pltpu.make_async_remote_copy(
            src_ref=origin,
            dst_ref=spot,
            send_sem=ys.at[which, dg - 1, k, ci],
            recv_sem=yr.at[which, dg - 1, k, ci],
            device_id=group(0, dg),
            device_id_type=MESH,
        )

    def forward(which, k, ci):
        for dg in range(1, ng):
            y_copy(which, k, ci, dg).start()

    def own_copy(which):
        start = pl.multiple_of((f * ng + g) * per_input, per_input)
        return pltpu.make_async_copy(
            sources[which].at[f], wholes[which].at[:, pl.ds(start, per_input), :], own_sem.at[which]
        )

    all_chunks = range(len(chunks))
    for which in (0, 1):
        for ci in all_chunks:
            for k in masks:
                z_copy(which, k, ci).start()
        if which == 0:
            for ci in all_chunks:
                forward(0, 0, ci)
    own_copy(0).start()
    own_copy(1).start()
    for ci in all_chunks:
        for k in masks:
            z_copy(0, k, ci).wait_recv()
            forward(0, k, ci)
    for ci in all_chunks:
        forward(1, 0, ci)
    own_copy(0).wait()
    for ci in all_chunks:
        for k in range(nf):
            for dg in range(1, ng):
                y_copy(0, k, ci, dg).wait_recv()

    scale = 1.0 / (samples * nt)
    row_start = pl.multiple_of(g * rows, rows)

    def vis_copy(i):
        return pltpu.make_async_remote_copy(
            src_ref=stage.at[i],
            dst_ref=landed.at[i],
            send_sem=vs.at[i],
            recv_sem=vr.at[i],
            device_id=group(i + 1, 0),
            device_id_type=MESH,
        )

    def correlate(i, carry):
        j = (t + 1 + i) % nt
        tile = pl.ds(pl.multiple_of(j * cols, cols), cols)
        mine_r = corr[0, pl.ds(row_start, rows), :]
        mine_i = corr[1, pl.ds(row_start, rows), :]
        other_r = corr[0, tile, :]
        other_i = corr[1, tile, :]
        real = (nt_dot(mine_r, other_r) + nt_dot(mine_i, other_i)) * scale
        imag = (nt_dot(mine_i, other_r) - nt_dot(mine_r, other_i)) * scale
        gram[0, :, tile] = real
        gram[1, :, tile] = imag

        @pl.when(i < nt - 1)
        def _():
            stage[i, 0] = real.astype(jnp.bfloat16)
            stage[i, 1] = imag.astype(jnp.bfloat16)
            vis_copy(i).start()

        return carry

    lax.fori_loop(0, nt, correlate, 0)

    pending = [(k, ci) for ci in all_chunks for k in masks]
    share = -(-len(pending) // (ITERS + 1))

    def relay(step):
        for k, ci in pending[step * share : (step + 1) * share]:
            z_copy(1, k, ci).wait_recv()
            forward(1, k, ci)

    z[...] = prior[0]
    slot = g * nt + t
    strip = LANES

    def update_copy(iteration, o):
        dt, dg = offsets[o]
        return pltpu.make_async_remote_copy(
            src_ref=updates.at[iteration, slot],
            dst_ref=updates.at[iteration, slot],
            send_sem=us.at[iteration, o],
            recv_sem=ur.at[iteration, o],
            device_id=group(dt, dg),
            device_id_type=MESH,
        )

    for iteration in range(ITERS):
        relay(iteration)
        power = jnp.sum(z[...] * z[...]) + 1e-06

        def product(r, carry):
            here = pl.ds(pl.multiple_of(r * strip, strip), strip)
            total_r = jnp.zeros((strip, LANES), jnp.float32)
            total_i = jnp.zeros((strip, LANES), jnp.float32)
            for c in range(inputs // LANES):
                lanes = slice(c * LANES, (c + 1) * LANES)
                part_r = gram[0, here, lanes]
                part_i = gram[1, here, lanes]
                gain_r = z[0:1, lanes]
                gain_i = z[1:2, lanes]
                total_r += part_r * gain_r - part_i * gain_i
                total_i += part_i * gain_r + part_r * gain_i
            updates[iteration, slot, 0:1, here] = jnp.sum(total_r.T, axis=0, keepdims=True)
            updates[iteration, slot, 1:2, here] = jnp.sum(total_i.T, axis=0, keepdims=True)
            return carry

        lax.fori_loop(0, rows // strip, product, 0)
        for o in range(len(offsets)):
            update_copy(iteration, o).start()
        for o in range(len(offsets)):
            update_copy(iteration, o).wait_recv()
        for h in range(ng):
            total = updates[iteration, h * nt]
            for other in range(1, nt):
                total = total + updates[iteration, h * nt + other]
            lanes = slice(h * rows, (h + 1) * rows)
            z[:, lanes] = 0.5 * (z[:, lanes] + inputs * total / power)

    gains[f] = z[...]
    gains_out[0] = z[...]

    def gain_copy(k):
        return pltpu.make_async_remote_copy(
            src_ref=gains.at[f],
            dst_ref=gains.at[f],
            send_sem=gs.at[k - 1],
            recv_sem=gr.at[k - 1],
            device_id=along_freq(k),
            device_id_type=MESH,
        )

    for k in masks:
        gain_copy(k).start()
    relay(ITERS)
    for k in masks:
        gain_copy(k).wait_recv()

    for i in range(nt - 1):
        vis_copy(i).wait_recv()
    own_tile = pl.ds(pl.multiple_of(t * cols, cols), cols)
    for part in (0, 1):
        total = gram[part, :, own_tile]
        for i in range(nt - 1):
            total = total + landed[i, part].astype(jnp.float32)
        vis_out[0, part] = total

    selected = onehot[0] * gains[0]
    for k in range(1, nf):
        selected = selected + onehot[k] * gains[k]

    own_copy(1).wait()
    for ci in all_chunks:
        for k in range(nf):
            for dg in range(1, ng):
                y_copy(1, k, ci, dg).wait_recv()

    beams = cosine.shape[0]
    factor = 1.0 / math.sqrt(half)
    cos = cosine[...]
    sin = sine[...]
    for p in (0, 1):
        gain_r = selected[0:1, p * half : (p + 1) * half]
        gain_i = selected[1:2, p * half : (p + 1) * half]
        denom = jnp.maximum(gain_r * gain_r + gain_i * gain_i, 0.5)
        along_r = gain_r / denom
        along_i = gain_i / denom
        w_r = (cos * along_r - sin * along_i) * factor
        w_i = -(cos * along_i + sin * along_r) * factor
        left = jnp.concatenate([w_r, w_i], axis=0).astype(jnp.bfloat16)
        right = jnp.concatenate([-w_i, w_r], axis=0).astype(jnp.bfloat16)
        result = jnp.dot(left, beam[0, p * half : (p + 1) * half, :], preferred_element_type=jnp.float32)
        result += jnp.dot(right, beam[1, p * half : (p + 1) * half, :], preferred_element_type=jnp.float32)
        result = result.astype(jnp.bfloat16)
        beams_out[0, p, 0] = result[:beams]
        beams_out[0, p, 1] = result[beams:]

    for which in (0, 1):
        for ci in all_chunks:
            for k in masks:
                z_copy(which, k, ci).wait_send()
            for k in range(nf):
                for dg in range(1, ng):
                    y_copy(which, k, ci, dg).wait_send()
    for i in range(nt - 1):
        vis_copy(i).wait_send()
    for iteration in range(ITERS):
        for o in range(len(offsets)):
            update_copy(iteration, o).wait_send()
    for k in masks:
        gain_copy(k).wait_send()


def body(
    voltages,
    prior_gains,
    station_flags,
    ingest_map,
    station_coords,
    pointing,
    corr_channels,
    beam_channels,
):
    nf = lax.axis_size("freq")
    nt = lax.axis_size("tm")
    ng = lax.axis_size("grp")
    f = lax.axis_index("freq")
    g = lax.axis_index("grp")
    channels, _, per_input, samples = voltages.shape
    stations = ingest_map.shape[0]
    inputs = 2 * stations
    rows, cols = inputs // ng, inputs // nt
    slot_keep = 1 - jnp.take(station_flags, ingest_map)
    keep = jnp.concatenate([slot_keep, slot_keep]).astype(jnp.bfloat16)
    mine = lax.dynamic_slice_in_dim(keep, (f * ng + g) * per_input, per_input)
    src_c = jnp.take(voltages, corr_channels, axis=0) * mine[None, None, :, None]
    src_b = jnp.take(voltages, beam_channels, axis=0) * mine[None, None, :, None]
    my_beam = lax.dynamic_slice_in_dim(beam_channels, f, 1, 0)
    onehot = (corr_channels == my_beam).astype(jnp.float32)
    ratio = 0.875 + 0.25 * (my_beam.astype(jnp.float32) + 0.5) / channels
    n_beams = pointing.shape[1] // ng
    pointing_part = lax.dynamic_slice_in_dim(pointing, g * n_beams, n_beams, 1)
    slot_coords = jnp.take(station_coords, ingest_map, axis=1)
    east = (pointing_part[0].astype(jnp.float32) + 0.5) / grid_cells - 0.5
    north = (pointing_part[1].astype(jnp.float32) + 0.5) / grid_cells - 0.5
    phase = 2.0 * math.pi * ratio * (
        east[:, None] * slot_coords[0][None, :] + north[:, None] * slot_coords[1][None, :]
    )
    step = min(per_input, 64)
    chunks = tuple((part, first, step) for first in range(0, per_input, step) for part in (0, 1))
    nc = len(chunks)
    dma = pltpu.SemaphoreType.DMA
    vmem = pl.BlockSpec(memory_space=pltpu.VMEM)
    vis, gains, beams = pl.pallas_call(
        functools.partial(kernel, nf, nt, ng, chunks),
        out_shape=(
            jax.ShapeDtypeStruct((1, 2, rows, cols), jnp.float32),
            jax.ShapeDtypeStruct((1, 2, inputs), jnp.float32),
            jax.ShapeDtypeStruct((1, 2, 2, n_beams, samples), jnp.bfloat16),
        ),
        in_specs=[vmem, vmem, vmem, pl.BlockSpec(memory_space=pltpu.SMEM), vmem, vmem],
        out_specs=(vmem, vmem, vmem),
        scratch_shapes=[
            pltpu.VMEM((2, inputs, samples), jnp.bfloat16),
            pltpu.VMEM((2, inputs, samples), jnp.bfloat16),
            pltpu.VMEM((2, rows, inputs), jnp.float32),
            pltpu.VMEM((nt, 2, rows, cols), jnp.bfloat16),
            pltpu.VMEM((nt - 1, 2, rows, cols), jnp.bfloat16),
            pltpu.VMEM((ITERS, ng * nt, 2, rows), jnp.float32),
            pltpu.VMEM((2, inputs), jnp.float32),
            pltpu.VMEM((nf, 2, inputs), jnp.float32),
            dma((2, nf - 1, nc)),
            dma((2, nf - 1, nc)),
            dma((2, ng - 1, nf, nc)),
            dma((2, ng - 1, nf, nc)),
            dma((2,)),
            dma((nt - 1,)),
            dma((nt - 1,)),
            dma((ITERS, ng * nt - 1)),
            dma((ITERS, ng * nt - 1)),
            dma((nf - 1,)),
            dma((nf - 1,)),
        ],
        compiler_params=pltpu.CompilerParams(
            collective_id=0, has_side_effects=True, vmem_limit_bytes=48 * 1024 * 1024
        ),
    )(src_c, src_b, prior_gains, onehot, jnp.cos(phase), jnp.sin(phase))
    return vis, gains, beams


def solution(mesh):
    return jax.shard_map(
        body,
        mesh=mesh,
        in_specs=(
            P(None, None, ("freq", "grp"), "tm"),
            P("freq", None, None),
            P(),
            P(),
            P(),
            P(),
            P(),
            P(),
        ),
        out_specs=(
            P("freq", None, "grp", "tm"),
            P("freq", None, None),
            P("freq", None, None, "grp", "tm"),
        ),
        check_vma=False,
    )
```

time: 315 us -> 169 us (0.54)
  blocking collectives: 159 us -> 0 us
  Pallas kernels: 0 us -> 145 us
  waiting for transfers between devices: 79.2 us -> 0 us
  matrix products: 24.5 us -> 0 us
  between operations: 17.3 us -> 1.4 us
  other arithmetic: 14.7 us -> 8.49 us
  local copies, waits for them, and re-layouts: 19 us -> 13.8 us
    pallas_call x0 -> x1, Pallas kernels: none -> 145 us  [body(): pl.pallas_call(functools.partial(kernel, nf, nt, ng, chunks), out_shape=(...]
    all_to_all x2 -> x0, blocking collectives: 105 us -> none  [the longest x1 54.4 us: body(): lax.all_to_all(corr_source, 'freq', split_axis=0, concat_axis=2, tiled=True)]
    reduce_scatter x1 -> x0, waiting for transfers between devices: 42.9 us -> none  [body(): lax.psum_scatter(partial_value, 'tm', scatter_dimension=3, tiled=True)]
    all_gather x2 -> x0, waiting for transfers between devices: 36.2 us -> none  [the longest x1 36.2 us: body(): lax.all_gather(beam_half.reshape(split_shape), 'grp', axis=3, tiled=True)]
    all_gather x5 -> x0, blocking collectives: 31 us -> none  [the longest x4 17.6 us: body(): gains = lax.all_gather(fresh, 'grp', axis=2, tiled=True)]
    dot_general x19 -> x0, matrix products: 24.5 us -> none  [the longest x1 6.13 us: body(): jnp.einsum('corit,crjt->coij', left, corr_volts, preferred_element_type=j...]
    psum x4 -> x0, blocking collectives: 22.8 us -> none  [body(): update = lax.psum(update, 'tm')]
    all_gather x2 -> x0, local copies, waits for them, and re-layouts: 5.04 us -> none  [the longest x1 4.6 us: body(): lax.all_gather(beam_half.reshape(split_shape), 'grp', axis=3, tiled=True)]
  transfers between devices with their start and end apart: 3 -> 0, of which waited for: 2 -> 0; matrix products, arithmetic and copies ran while one was open for 9% -> 0% of each run, Pallas kernels for 0% -> 0%
where the time goes in v1:
time: 169 us
  Pallas kernels  145 us (86%)
  local copies, waits for them, and re-layouts  13.8 us (8%)
  other arithmetic  8.49 us (5%)
    pallas_call x1, Pallas kernels, body(): pl.pallas_call(functools.partial(kernel, nf, nt, ng, chunks), out_shape=(...  145 us
    mul x1, other arithmetic, body(): jnp.take(voltages, beam_channels, axis=0) * mine[None, None, :, None]  3.97 us
    gather x1, local copies, waits for them, and re-layouts, body(): slot_keep = 1 - jnp.take(station_flags, ingest_map)  3.62 us

profile of v1, /device:TPU:0, one launch (start us, length us, event | category | flops | bytes accessed | tf_op | source)
XLA Modules:
  0.0 168.8 jit_solution(5776579814559756344)
XLA Ops:
  0.6 0.0 copy-start
  0.6 0.0 copy-start.2
  0.7 0.0 copy-start.3
  0.7 1.4 dynamic_slice.10
  2.7 0.7 constant_dynamic-slice_fusion
  3.4 0.7 compare_select_fusion.2
  4.1 0.7 compare_select_fusion.1
  4.7 1.3 compare_convert_fusion
  6.1 0.7 compare_select_fusion
  6.8 3.6 %gather_fusion = s32[512]{0:T(512)S(1)} fusion(s32[512]{0:T(512)} %param.12, s32[1024]{0:T(1024)S(1)} %pad_clamp_fusion.1), kind=kCustom, calls=%fused_computation.2 | custom fusion | bytes 6144 | tf_op jit(solution)/shard_map/jit(_take)/gather | solution.py:336
  10.4 0.0 copy-done.2
  10.4 0.1 dynamic_slice.9
  10.5 0.0 copy-done.3
  10.5 0.1 copy.12
  10.7 1.0 gather_fusion.1
  11.7 0.1 select_bitcast_fusion
  11.8 0.3 slice_reduce_fusion.1
  12.2 1.0 fusion
  13.2 0.0 copy-done
  13.2 2.0 %gather_fusion.2 = bf16[4,2,128,1024]{3,2,1,0:T(8,128)(2,1)} fusion(bf16[4,2,128,1024]{3,2,1,0:T(8,128)(2,1)S(1)} %copy-done, s32[1024]{0:T(1024)S(1)} %pad_clamp_fusion.2), kind=kCustom, calls=%fused_computation.clone | custom fusion | bytes 4194320 | tf_op jit(solution)/shard_map/jit(_take)/gather | solution.py:339
  15.2 2.0 %gather_fusion.3 = bf16[4,2,128,1024]{3,2,1,0:T(8,128)(2,1)} fusion(bf16[4,2,128,1024]{3,2,1,0:T(8,128)(2,1)S(1)} %copy-done, s32[1024]{0:T(1024)S(1)} %pad_clamp_fusion), kind=kCustom, calls=%fused_computation.1.clone | custom fusion | bytes 4194320 | tf_op jit(solution)/shard_map/jit(_take)/gather | solution.py:340
  17.2 0.0 copy-start.1
  17.2 4.0 %select_multiply_fusion = (bf16[4,2,128,1024]{3,2,1,0:T(8,128)(2,1)}, bf16[4,2,128,1024]{3,2,1,0:T(8,128)(2,1)S(1)}) fusion(bf16[4,2,128,1024]{3,2,1,0:T(8,128)(2,1)} %gather_fusion.3, pred[4]{0:T(512)(128)(4,1)S(1)} %get-tuple-element.16, bf16[128]{0:T(256)(128)(2,1)S(1)} %dynamic_slice.9, bf16[4,2,128,1024]{3,2,1,0:T(8,128)(2,1)} %gather_fusion.2, ...), kind=kLoop, calls=%fused_computation.4 | loop fusion | flops 4194304 | bytes 8388872 | tf_op jit(solution)/shard_map/mul | solution.py:340
  21.2 0.0 copy-done.1
  21.2 145.1 %shard_map.103 = (f32[1,2,512,256]{3,2,1,0:T(8,128)S(1)}, f32[1,2,1024]{2,1,0:T(2,128)S(1)}, bf16[1,2,2,128,1024]{4,3,2,1,0:T(8,128)(2,1)S(1)}) custom-call(bf16[4,2,128,1024]{3,2,1,0:T(8,128)(2,1)S(1)} %get-tuple-element.15.src_c, bf16[4,2,128,1024]{3,2,1,0:T(8,128)(2,1)} %get-tuple-element.14.src_b, f32[1,2,1024]{2,1,0:T(2,128)S(1)} %copy-done.1, ...), custom_call_target="tpu_custom_call" | custom-call | tf_op jit(solution)/shard_map/pallas_call | solution.py:357
  166.2 1.0 copy.16
  167.2 0.6 copy.17
  167.8 1.0 copy.18
  (6 shorter events, 0.0 us)
Async XLA Ops:
  0.6 12.5 %copy-start = (bf16[4,2,128,1024]{3,2,1,0:T(8,128)(2,1)S(1)}, bf16[4,2,128,1024]{3,2,1,0:T(8,128)(2,1)}, u32[]{:S(2)}) copy-start(bf16[4,2,128,1024]{3,2,1,0:T(8,128)(2,1)} %param.10) | copy-start | bytes 6291460
  0.6 9.7 %copy-start.2 = (s32[512]{0:T(512)S(1)}, s32[512]{0:T(512)}, u32[]{:S(2)}) copy-start(s32[512]{0:T(512)} %param.13) | copy-start | bytes 6148
  0.7 9.8 %copy-start.3 = (f32[2,512]{1,0:T(2,128)S(1)}, f32[2,512]{1,0:T(2,128)}, u32[]{:S(2)}) copy-start(f32[2,512]{1,0:T(2,128)} %param.14) | copy-start | bytes 12292
  17.2 4.0 %copy-start.1 = (f32[1,2,1024]{2,1,0:T(2,128)S(1)}, f32[1,2,1024]{2,1,0:T(2,128)}, u32[]{:S(2)}) copy-start(f32[1,2,1024]{2,1,0:T(2,128)} %prior.1) | copy-start | bytes 24580

commit v2 on v1

--- a/solution.py
+++ b/solution.py
@@ -32,15 +32,22 @@
     nt,
     ng,
     chunks,
-    src_c,
-    src_b,
+    voltages,
     prior,
-    onehot,
-    cosine,
-    sine,
+    flags,
+    slots,
+    coords,
+    pointing,
+    corr_channels,
+    beam_channels,
     vis_out,
     gains_out,
     beams_out,
+    src_c,
+    src_b,
+    keep,
+    cosine,
+    sine,
     corr,
     beam,
     gram,
@@ -64,7 +71,7 @@
     f = lax.axis_index("freq")
     t = lax.axis_index("tm")
     g = lax.axis_index("grp")
-    _, _, per_input, samples = src_c.shape
+    _, _, per_input, samples = voltages.shape
     inputs = nf * ng * per_input
     rows = inputs // ng
     cols = inputs // nt
@@ -79,11 +86,30 @@
     def along_freq(k):
         return {"freq": peers[k], "tm": t, "grp": g}
 
+    stations = half
+    slot_rows = jnp.broadcast_to(slots[...].astype(jnp.float32), (LANES, stations)).T
+    flagged = jnp.zeros((stations, LANES), jnp.float32)
+    for first in range(0, stations, LANES):
+        lane = lax.broadcasted_iota(jnp.int32, (stations, LANES), 1) + first
+        flag = flags[0:1, first : first + LANES].astype(jnp.float32)
+        flagged += jnp.where(slot_rows == lane.astype(jnp.float32), flag, 0.0)
+    flagged = jnp.sum(flagged, axis=1, keepdims=True)
+    keep[...] = jnp.broadcast_to(1.0 - flagged, (stations, LANES))
+
     barrier = pltpu.get_barrier_semaphore()
     for k in masks:
         pl.semaphore_signal(barrier, inc=1, device_id=along_freq(k), device_id_type=MESH)
     for dt, dg in offsets:
         pl.semaphore_signal(barrier, inc=1, device_id=group(dt, dg), device_id_type=MESH)
+    first_slot = pl.multiple_of(((f * ng + g) * per_input) % stations, per_input)
+    kept = keep[pl.ds(first_slot, per_input), 0:1].astype(jnp.bfloat16)
+
+    def pick(source, channels):
+        for k in masks + [0]:
+            for part in (0, 1):
+                source[peers[k], part] = voltages[channels[peers[k]], part] * kept
+
+    pick(src_c, corr_channels)
     pl.semaphore_wait(barrier, len(masks) + len(offsets))
 
     sources = (src_c, src_b)
@@ -128,15 +154,39 @@
             sources[which].at[f], wholes[which].at[:, pl.ds(start, per_input), :], own_sem.at[which]
         )
 
+    beams = cosine.shape[0]
+    my_beam = beam_channels[f]
+
+    def point_phases():
+        ratio = 0.875 + 0.25 * (my_beam.astype(jnp.float32) + 0.5) / nf
+        here = pl.ds(pl.multiple_of(g * beams, beams), beams)
+        east_dir, north_dir = (
+            jnp.broadcast_to((pointing[d : d + 1, here].astype(jnp.float32) + 0.5) / grid_cells - 0.5, (LANES, beams)).T
+            for d in (0, 1)
+        )
+        east, north = (jnp.broadcast_to(coords[d : d + 1, :], (LANES, stations)).T for d in (0, 1))
+        station = lax.broadcasted_iota(jnp.int32, (stations, LANES), 0)
+        for first in range(0, stations, LANES):
+            lanes = slice(first, first + LANES)
+            match = station == slots[0:1, lanes]
+            slot_east = jnp.sum(jnp.where(match, east, 0.0), axis=0, keepdims=True)
+            slot_north = jnp.sum(jnp.where(match, north, 0.0), axis=0, keepdims=True)
+            phase = 2.0 * math.pi * ratio * (east_dir * slot_east + north_dir * slot_north)
+            cosine[:, lanes] = jnp.cos(phase)
+            sine[:, lanes] = jnp.sin(phase)
+
     all_chunks = range(len(chunks))
-    for which in (0, 1):
-        for ci in all_chunks:
-            for k in masks:
-                z_copy(which, k, ci).start()
-        if which == 0:
-            for ci in all_chunks:
-                forward(0, 0, ci)
+    for ci in all_chunks:
+        for k in masks:
+            z_copy(0, k, ci).start()
+    for ci in all_chunks:
+        forward(0, 0, ci)
     own_copy(0).start()
+    pick(src_b, beam_channels)
+    point_phases()
+    for ci in all_chunks:
+        for k in masks:
+            z_copy(1, k, ci).start()
     own_copy(1).start()
     for ci in all_chunks:
         for k in masks:
@@ -268,9 +318,9 @@
             total = total + landed[i, part].astype(jnp.float32)
         vis_out[0, part] = total
 
-    selected = onehot[0] * gains[0]
-    for k in range(1, nf):
-        selected = selected + onehot[k] * gains[k]
+    selected = jnp.zeros_like(z)
+    for k in range(nf):
+        selected = selected + jnp.where(corr_channels[k] == my_beam, 1.0, 0.0) * gains[k]
 
     own_copy(1).wait()
     for ci in all_chunks:
@@ -278,7 +328,6 @@
             for dg in range(1, ng):
                 y_copy(1, k, ci, dg).wait_recv()
 
-    beams = cosine.shape[0]
     factor = 1.0 / math.sqrt(half)
     cos = cosine[...]
     sin = sine[...]
@@ -327,28 +376,11 @@
     nf = lax.axis_size("freq")
     nt = lax.axis_size("tm")
     ng = lax.axis_size("grp")
-    f = lax.axis_index("freq")
-    g = lax.axis_index("grp")
-    channels, _, per_input, samples = voltages.shape
+    _, _, per_input, samples = voltages.shape
     stations = ingest_map.shape[0]
     inputs = 2 * stations
     rows, cols = inputs // ng, inputs // nt
-    slot_keep = 1 - jnp.take(station_flags, ingest_map)
-    keep = jnp.concatenate([slot_keep, slot_keep]).astype(jnp.bfloat16)
-    mine = lax.dynamic_slice_in_dim(keep, (f * ng + g) * per_input, per_input)
-    src_c = jnp.take(voltages, corr_channels, axis=0) * mine[None, None, :, None]
-    src_b = jnp.take(voltages, beam_channels, axis=0) * mine[None, None, :, None]
-    my_beam = lax.dynamic_slice_in_dim(beam_channels, f, 1, 0)
-    onehot = (corr_channels == my_beam).astype(jnp.float32)
-    ratio = 0.875 + 0.25 * (my_beam.astype(jnp.float32) + 0.5) / channels
     n_beams = pointing.shape[1] // ng
-    pointing_part = lax.dynamic_slice_in_dim(pointing, g * n_beams, n_beams, 1)
-    slot_coords = jnp.take(station_coords, ingest_map, axis=1)
-    east = (pointing_part[0].astype(jnp.float32) + 0.5) / grid_cells - 0.5
-    north = (pointing_part[1].astype(jnp.float32) + 0.5) / grid_cells - 0.5
-    phase = 2.0 * math.pi * ratio * (
-        east[:, None] * slot_coords[0][None, :] + north[:, None] * slot_coords[1][None, :]
-    )
     step = min(per_input, 64)
     chunks = tuple((part, first, step) for first in range(0, per_input, step) for part in (0, 1))
     nc = len(chunks)
@@ -361,9 +393,14 @@
             jax.ShapeDtypeStruct((1, 2, inputs), jnp.float32),
             jax.ShapeDtypeStruct((1, 2, 2, n_beams, samples), jnp.bfloat16),
         ),
-        in_specs=[vmem, vmem, vmem, pl.BlockSpec(memory_space=pltpu.SMEM), vmem, vmem],
+        in_specs=[vmem] * 6 + [pl.BlockSpec(memory_space=pltpu.SMEM)] * 2,
         out_specs=(vmem, vmem, vmem),
         scratch_shapes=[
+            pltpu.VMEM((nf, 2, per_input, samples), jnp.bfloat16),
+            pltpu.VMEM((nf, 2, per_input, samples), jnp.bfloat16),
+            pltpu.VMEM((stations, LANES), jnp.float32),
+            pltpu.VMEM((n_beams, stations), jnp.float32),
+            pltpu.VMEM((n_beams, stations), jnp.float32),
             pltpu.VMEM((2, inputs, samples), jnp.bfloat16),
             pltpu.VMEM((2, inputs, samples), jnp.bfloat16),
             pltpu.VMEM((2, rows, inputs), jnp.float32),
@@ -387,7 +424,16 @@
         compiler_params=pltpu.CompilerParams(
             collective_id=0, has_side_effects=True, vmem_limit_bytes=48 * 1024 * 1024
         ),
-    )(src_c, src_b, prior_gains, onehot, jnp.cos(phase), jnp.sin(phase))
+    )(
+        voltages,
+        prior_gains,
+        station_flags[None],
+        ingest_map[None],
+        station_coords,
+        pointing,
+        corr_channels,
+        beam_channels,
+    )
     return vis, gains, beams
 
 

time: 169 us -> 154 us (0.911)
  other arithmetic: 8.49 us -> 0 us
  local copies, waits for them, and re-layouts: 13.8 us -> 8.86 us
    gather x4 -> x0, local copies, waits for them, and re-layouts: 8.66 us -> none  [the longest x1 3.62 us: body(): slot_keep = 1 - jnp.take(station_flags, ingest_map)]
    unnamed x12 -> x19, local copies, waits for them, and re-layouts: 2.71 us -> 8.86 us
    mul x1 -> x0, other arithmetic: 3.97 us -> none  [body(): jnp.take(voltages, beam_channels, axis=0) * mine[None, None, :, None]]
    dynamic_slice x3 -> x0, local copies, waits for them, and re-layouts: 2.15 us -> none  [the longest x1 1.38 us: body(): my_beam = lax.dynamic_slice_in_dim(beam_channels, f, 1, 0)]
    select_n x4 -> x0, other arithmetic: 2.14 us -> none  [the longest x1 0.68 us: body(): slot_keep = 1 - jnp.take(station_flags, ingest_map)]
where the time goes in v2:
time: 154 us
  Pallas kernels  144 us (94%)
  local copies, waits for them, and re-layouts  8.86 us (6%)
    pallas_call x1, Pallas kernels, body(): pl.pallas_call(functools.partial(kernel, nf, nt, ng, chunks), out_shape=(...  144 us
    unnamed x19, local copies, waits for them, and re-layouts  8.86 us

profile of v2, /device:TPU:0, one launch (start us, length us, event | category | flops | bytes accessed | tf_op | source)
XLA Modules:
  0.0 153.7 jit_solution(3364636354795884596)
XLA Ops:
  0.6 0.0 copy-start
  0.6 1.6 %copy-done = bf16[4,2,128,1024]{3,2,1,0:T(8,128)(2,1)S(1)} copy-done((bf16[4,2,128,1024]{3,2,1,0:T(8,128)(2,1)S(1)}, bf16[4,2,128,1024]{3,2,1,0:T(8,128)(2,1)}, u32[]{:S(2)}) %copy-start) | copy-done | bytes 2097176
  2.2 0.0 copy-start.1
  2.2 0.7 copy-done.1
  2.9 0.0 copy-start.2
  2.9 0.7 copy-done.2
  3.6 0.0 copy-start.3
  3.6 0.7 copy-done.3
  4.3 0.0 copy-start.4
  4.3 0.7 copy-done.4
  5.0 0.0 copy-start.5
  5.0 0.7 copy-done.5
  5.7 0.0 copy-start.6
  5.7 0.7 copy-done.6
  6.3 0.0 copy-start.7
  6.3 0.7 copy-done.7
  7.0 144.2 %shard_map.103 = (f32[1,2,512,256]{3,2,1,0:T(8,128)S(1)}, f32[1,2,1024]{2,1,0:T(2,128)S(1)}, bf16[1,2,2,128,1024]{4,3,2,1,0:T(8,128)(2,1)S(1)}) custom-call(bf16[4,2,128,1024]{3,2,1,0:T(8,128)(2,1)S(1)} %copy-done, f32[1,2,1024]{2,1,0:T(2,128)S(1)} %copy-done.1, s32[1,512]{1,0:T(1,128)S(1)} %bitcast.2, s32[1,512]{1,0:T(1,128)S(1)} %bitcast.3, ...), custom_call_target="tpu_custom_call" | custom-call | tf_op jit(solution)/shard_map/pallas_call | solution.py:389
  151.2 1.0 copy.14
  152.1 0.6 copy.15
  152.7 1.0 copy.16
Async XLA Ops:
  0.6 1.6 %copy-start = (bf16[4,2,128,1024]{3,2,1,0:T(8,128)(2,1)S(1)}, bf16[4,2,128,1024]{3,2,1,0:T(8,128)(2,1)}, u32[]{:S(2)}) copy-start(bf16[4,2,128,1024]{3,2,1,0:T(8,128)(2,1)} %voltages.1) | copy-start | bytes 6291460
  2.2 0.7 copy-start.1
  2.9 0.7 copy-start.2
  3.6 0.7 copy-start.3
  4.3 0.7 copy-start.4
  5.0 0.7 copy-start.5
  5.7 0.7 copy-start.6
  6.3 0.7 copy-start.7

commit v3 on v2

--- a/solution.py
+++ b/solution.py
@@ -32,42 +32,54 @@
     nt,
     ng,
     chunks,
-    voltages,
-    prior,
-    flags,
-    slots,
-    coords,
-    pointing,
-    corr_channels,
-    beam_channels,
-    vis_out,
-    gains_out,
-    beams_out,
-    src_c,
-    src_b,
-    keep,
-    cosine,
-    sine,
-    corr,
-    beam,
-    gram,
-    stage,
-    landed,
-    updates,
-    z,
-    gains,
-    zs,
-    zr,
-    ys,
-    yr,
-    own_sem,
-    vs,
-    vr,
-    us,
-    ur,
-    gs,
-    gr,
+    windows,
+    *refs,
 ):
+    operands, refs = refs[:8], refs[8:]
+    (
+        vis_out,
+        gains_out,
+        beams_out,
+        src_c,
+        src_b,
+        keep,
+        cosine,
+        sine,
+        left,
+        right,
+        mine_beams,
+        sent_beams,
+        got_beams,
+        corr,
+        beam,
+        gram,
+        stage,
+        landed,
+        updates,
+        z,
+        gains,
+        zs,
+        zr,
+        ys,
+        yr,
+        bs,
+        br,
+        ps,
+        pr,
+        own_sem,
+        vs,
+        vr,
+        us,
+        ur,
+        gs,
+        gr,
+        in_sem,
+    ) = refs[:-8]
+    held = refs[-8:]
+    voltages, prior, flags, slots, coords, pointing, corr_channels, beam_channels = held
+    loads = [pltpu.make_async_copy(operands[i], held[i], in_sem.at[i]) for i in range(8)]
+    for load in loads:
+        load.start()
     f = lax.axis_index("freq")
     t = lax.axis_index("tm")
     g = lax.axis_index("grp")
@@ -86,6 +98,13 @@
     def along_freq(k):
         return {"freq": peers[k], "tm": t, "grp": g}
 
+    barrier = pltpu.get_barrier_semaphore()
+    for k in masks:
+        pl.semaphore_signal(barrier, inc=1, device_id=along_freq(k), device_id_type=MESH)
+    for dt, dg in offsets:
+        pl.semaphore_signal(barrier, inc=1, device_id=group(dt, dg), device_id_type=MESH)
+    for load in loads:
+        load.wait()
     stations = half
     slot_rows = jnp.broadcast_to(slots[...].astype(jnp.float32), (LANES, stations)).T
     flagged = jnp.zeros((stations, LANES), jnp.float32)
@@ -96,72 +115,99 @@
     flagged = jnp.sum(flagged, axis=1, keepdims=True)
     keep[...] = jnp.broadcast_to(1.0 - flagged, (stations, LANES))
 
-    barrier = pltpu.get_barrier_semaphore()
-    for k in masks:
-        pl.semaphore_signal(barrier, inc=1, device_id=along_freq(k), device_id_type=MESH)
-    for dt, dg in offsets:
-        pl.semaphore_signal(barrier, inc=1, device_id=group(dt, dg), device_id_type=MESH)
     first_slot = pl.multiple_of(((f * ng + g) * per_input) % stations, per_input)
     kept = keep[pl.ds(first_slot, per_input), 0:1].astype(jnp.bfloat16)
 
-    def pick(source, channels):
-        for k in masks + [0]:
-            for part in (0, 1):
-                source[peers[k], part] = voltages[channels[peers[k]], part] * kept
-
-    pick(src_c, corr_channels)
+    for k in masks + [0]:
+        for part in (0, 1):
+            src_c[peers[k], part] = voltages[corr_channels[peers[k]], part] * kept
+
     pl.semaphore_wait(barrier, len(masks) + len(offsets))
-
-    sources = (src_c, src_b)
-    wholes = (corr, beam)
-
-    def place(whole, owner, chunk):
+    nw = windows
+    width = samples // nw
+
+    def place(owner, chunk):
         part, first, count = chunk
         start = pl.multiple_of((owner * ng + g) * per_input + first, count)
-        return whole.at[part, pl.ds(start, count), :]
-
-    def z_copy(which, k, ci):
+        return corr.at[part, pl.ds(start, count), :]
+
+    def z_copy(k, ci):
         part, first, count = chunks[ci]
         return pltpu.make_async_remote_copy(
-            src_ref=sources[which].at[peers[k], part, pl.ds(first, count), :],
-            dst_ref=place(wholes[which], f, chunks[ci]),
-            send_sem=zs.at[which, k - 1, ci],
-            recv_sem=zr.at[which, k - 1, ci],
+            src_ref=src_c.at[peers[k], part, pl.ds(first, count), :],
+            dst_ref=place(f, chunks[ci]),
+            send_sem=zs.at[k - 1, ci],
+            recv_sem=zr.at[k - 1, ci],
             device_id=along_freq(k),
             device_id_type=MESH,
         )
 
-    def y_copy(which, k, ci, dg):
+    def y_copy(k, ci, dg):
         part, first, count = chunks[ci]
-        spot = place(wholes[which], peers[k], chunks[ci])
-        origin = sources[which].at[f, part, pl.ds(first, count), :] if k == 0 else spot
-        return pltpu.make_async_remote_copy(
-            src_ref=origin,
+        spot = place(peers[k], chunks[ci])
+        return pltpu.make_async_remote_copy(
+            src_ref=src_c.at[f, part, pl.ds(first, count), :] if k == 0 else spot,
             dst_ref=spot,
-            send_sem=ys.at[which, dg - 1, k, ci],
-            recv_sem=yr.at[which, dg - 1, k, ci],
+            send_sem=ys.at[dg - 1, k, ci],
+            recv_sem=yr.at[dg - 1, k, ci],
             device_id=group(0, dg),
             device_id_type=MESH,
         )
 
-    def forward(which, k, ci):
+    def forward(k, ci):
         for dg in range(1, ng):
-            y_copy(which, k, ci, dg).start()
-
-    def own_copy(which):
-        start = pl.multiple_of((f * ng + g) * per_input, per_input)
-        return pltpu.make_async_copy(
-            sources[which].at[f], wholes[which].at[:, pl.ds(start, per_input), :], own_sem.at[which]
-        )
-
-    beams = cosine.shape[0]
+            y_copy(k, ci, dg).start()
+
+    def block(owner, member):
+        return pl.ds(pl.multiple_of((owner * ng + member) * per_input, per_input), per_input)
+
+    own_copy = pltpu.make_async_copy(src_c.at[f], corr.at[:, block(f, g), :], own_sem)
+
+    def b_copy(k, w):
+        return pltpu.make_async_remote_copy(
+            src_ref=src_b.at[peers[k], w],
+            dst_ref=beam.at[w, :, block(f, g), :],
+            send_sem=bs.at[k - 1, w],
+            recv_sem=br.at[k - 1, w],
+            device_id=along_freq(k),
+            device_id_type=MESH,
+        )
+
+    def p_copy(dg, w):
+        return pltpu.make_async_remote_copy(
+            src_ref=sent_beams.at[dg - 1, w],
+            dst_ref=got_beams.at[dg - 1, w],
+            send_sem=ps.at[dg - 1, w],
+            recv_sem=pr.at[dg - 1, w],
+            device_id=group(0, dg),
+            device_id_type=MESH,
+        )
+
+    def pick_beams():
+        for w in range(nw):
+            for k in masks + [0]:
+                for part in (0, 1):
+                    picked = voltages[beam_channels[peers[k]], part, :, w * width : (w + 1) * width] * kept
+                    if k == 0:
+                        beam[w, part, block(f, g), :] = picked
+                    else:
+                        src_b[peers[k], w, part] = picked
+
+    def clear_others():
+        for w in range(nw):
+            for owner in range(nf):
+                for dg in range(1, ng):
+                    for part in (0, 1):
+                        beam[w, part, block(owner, (g + dg) % ng), :] = jnp.zeros((per_input, width), jnp.bfloat16)
+
+    n_beams = cosine.shape[0]
+    beams = n_beams // ng
     my_beam = beam_channels[f]
 
     def point_phases():
         ratio = 0.875 + 0.25 * (my_beam.astype(jnp.float32) + 0.5) / nf
-        here = pl.ds(pl.multiple_of(g * beams, beams), beams)
         east_dir, north_dir = (
-            jnp.broadcast_to((pointing[d : d + 1, here].astype(jnp.float32) + 0.5) / grid_cells - 0.5, (LANES, beams)).T
+            jnp.broadcast_to((pointing[d : d + 1, :].astype(jnp.float32) + 0.5) / grid_cells - 0.5, (LANES, n_beams)).T
             for d in (0, 1)
         )
         east, north = (jnp.broadcast_to(coords[d : d + 1, :], (LANES, stations)).T for d in (0, 1))
@@ -178,27 +224,25 @@
     all_chunks = range(len(chunks))
     for ci in all_chunks:
         for k in masks:
-            z_copy(0, k, ci).start()
+            z_copy(k, ci).start()
     for ci in all_chunks:
-        forward(0, 0, ci)
-    own_copy(0).start()
-    pick(src_b, beam_channels)
+        forward(0, ci)
+    own_copy.start()
+    pick_beams()
+    for w in range(nw):
+        for k in masks:
+            b_copy(k, w).start()
+    clear_others()
     point_phases()
     for ci in all_chunks:
         for k in masks:
-            z_copy(1, k, ci).start()
-    own_copy(1).start()
-    for ci in all_chunks:
-        for k in masks:
-            z_copy(0, k, ci).wait_recv()
-            forward(0, k, ci)
-    for ci in all_chunks:
-        forward(1, 0, ci)
-    own_copy(0).wait()
+            z_copy(k, ci).wait_recv()
+            forward(k, ci)
+    own_copy.wait()
     for ci in all_chunks:
         for k in range(nf):
             for dg in range(1, ng):
-                y_copy(0, k, ci, dg).wait_recv()
+                y_copy(k, ci, dg).wait_recv()
 
     scale = 1.0 / (samples * nt)
     row_start = pl.multiple_of(g * rows, rows)
@@ -235,14 +279,6 @@
 
     lax.fori_loop(0, nt, correlate, 0)
 
-    pending = [(k, ci) for ci in all_chunks for k in masks]
-    share = -(-len(pending) // (ITERS + 1))
-
-    def relay(step):
-        for k, ci in pending[step * share : (step + 1) * share]:
-            z_copy(1, k, ci).wait_recv()
-            forward(1, k, ci)
-
     z[...] = prior[0]
     slot = g * nt + t
     strip = LANES
@@ -259,7 +295,6 @@
         )
 
     for iteration in range(ITERS):
-        relay(iteration)
         power = jnp.sum(z[...] * z[...]) + 1e-06
 
         def product(r, carry):
@@ -305,10 +340,6 @@
 
     for k in masks:
         gain_copy(k).start()
-    relay(ITERS)
-    for k in masks:
-        gain_copy(k).wait_recv()
-
     for i in range(nt - 1):
         vis_copy(i).wait_recv()
     own_tile = pl.ds(pl.multiple_of(t * cols, cols), cols)
@@ -318,42 +349,68 @@
             total = total + landed[i, part].astype(jnp.float32)
         vis_out[0, part] = total
 
+    for k in masks:
+        gain_copy(k).wait_recv()
     selected = jnp.zeros_like(z)
     for k in range(nf):
         selected = selected + jnp.where(corr_channels[k] == my_beam, 1.0, 0.0) * gains[k]
 
-    own_copy(1).wait()
-    for ci in all_chunks:
-        for k in range(nf):
-            for dg in range(1, ng):
-                y_copy(1, k, ci, dg).wait_recv()
-
     factor = 1.0 / math.sqrt(half)
-    cos = cosine[...]
-    sin = sine[...]
     for p in (0, 1):
         gain_r = selected[0:1, p * half : (p + 1) * half]
         gain_i = selected[1:2, p * half : (p + 1) * half]
         denom = jnp.maximum(gain_r * gain_r + gain_i * gain_i, 0.5)
         along_r = gain_r / denom
         along_i = gain_i / denom
-        w_r = (cos * along_r - sin * along_i) * factor
-        w_i = -(cos * along_i + sin * along_r) * factor
-        left = jnp.concatenate([w_r, w_i], axis=0).astype(jnp.bfloat16)
-        right = jnp.concatenate([-w_i, w_r], axis=0).astype(jnp.bfloat16)
-        result = jnp.dot(left, beam[0, p * half : (p + 1) * half, :], preferred_element_type=jnp.float32)
-        result += jnp.dot(right, beam[1, p * half : (p + 1) * half, :], preferred_element_type=jnp.float32)
-        result = result.astype(jnp.bfloat16)
-        beams_out[0, p, 0] = result[:beams]
-        beams_out[0, p, 1] = result[beams:]
-
-    for which in (0, 1):
-        for ci in all_chunks:
-            for k in masks:
-                z_copy(which, k, ci).wait_send()
-            for k in range(nf):
-                for dg in range(1, ng):
-                    y_copy(which, k, ci, dg).wait_send()
+        for h in range(ng):
+            span = slice(h * beams, (h + 1) * beams)
+            cos = cosine[span, :]
+            sin = sine[span, :]
+            w_r = ((cos * along_r - sin * along_i) * factor).astype(jnp.bfloat16)
+            w_i = (-(cos * along_i + sin * along_r) * factor).astype(jnp.bfloat16)
+            left[p, h, 0:beams] = w_r
+            left[p, h, beams:] = w_i
+            right[p, h, 0:beams] = -w_i
+            right[p, h, beams:] = w_r
+
+    def beamform(p, w, side):
+        rows_p = slice(p * half, (p + 1) * half)
+        result = jnp.dot(left[p, side], beam[w, 0, rows_p, :], preferred_element_type=jnp.float32)
+        return result + jnp.dot(right[p, side], beam[w, 1, rows_p, :], preferred_element_type=jnp.float32)
+
+    for w in range(nw):
+        for k in masks:
+            b_copy(k, w).wait_recv()
+        for dg in range(1, ng):
+            for p in (0, 1):
+                sent_beams[dg - 1, w, p] = beamform(p, w, (g + dg) % ng).astype(jnp.bfloat16)
+            p_copy(dg, w).start()
+        for p in (0, 1):
+            mine_beams[w, p] = beamform(p, w, g)
+
+    for w in range(nw):
+        lanes = slice(w * width, (w + 1) * width)
+        for dg in range(1, ng):
+            p_copy(dg, w).wait_recv()
+        for p in (0, 1):
+            total = mine_beams[w, p]
+            for dg in range(1, ng):
+                total = total + got_beams[dg - 1, w, p].astype(jnp.float32)
+            total = total.astype(jnp.bfloat16)
+            beams_out[0, p, 0, :, lanes] = total[:beams]
+            beams_out[0, p, 1, :, lanes] = total[beams:]
+
+    for ci in all_chunks:
+        for k in masks:
+            z_copy(k, ci).wait_send()
+        for k in range(nf):
+            for dg in range(1, ng):
+                y_copy(k, ci, dg).wait_send()
+    for w in range(nw):
+        for k in masks:
+            b_copy(k, w).wait_send()
+        for dg in range(1, ng):
+            p_copy(dg, w).wait_send()
     for i in range(nt - 1):
         vis_copy(i).wait_send()
     for iteration in range(ITERS):
@@ -380,46 +437,67 @@
     stations = ingest_map.shape[0]
     inputs = 2 * stations
     rows, cols = inputs // ng, inputs // nt
-    n_beams = pointing.shape[1] // ng
-    step = min(per_input, 64)
+    n_beams = pointing.shape[1]
+    part_beams = n_beams // ng
+    nw = 4
+    width = samples // nw
+    step = min(per_input, 32)
     chunks = tuple((part, first, step) for first in range(0, per_input, step) for part in (0, 1))
     nc = len(chunks)
     dma = pltpu.SemaphoreType.DMA
     vmem = pl.BlockSpec(memory_space=pltpu.VMEM)
     vis, gains, beams = pl.pallas_call(
-        functools.partial(kernel, nf, nt, ng, chunks),
+        functools.partial(kernel, nf, nt, ng, chunks, nw),
         out_shape=(
             jax.ShapeDtypeStruct((1, 2, rows, cols), jnp.float32),
             jax.ShapeDtypeStruct((1, 2, inputs), jnp.float32),
-            jax.ShapeDtypeStruct((1, 2, 2, n_beams, samples), jnp.bfloat16),
+            jax.ShapeDtypeStruct((1, 2, 2, part_beams, samples), jnp.bfloat16),
         ),
-        in_specs=[vmem] * 6 + [pl.BlockSpec(memory_space=pltpu.SMEM)] * 2,
+        in_specs=[pl.BlockSpec(memory_space=pltpu.HBM)] * 8,
         out_specs=(vmem, vmem, vmem),
         scratch_shapes=[
             pltpu.VMEM((nf, 2, per_input, samples), jnp.bfloat16),
-            pltpu.VMEM((nf, 2, per_input, samples), jnp.bfloat16),
+            pltpu.VMEM((nf, nw, 2, per_input, width), jnp.bfloat16),
             pltpu.VMEM((stations, LANES), jnp.float32),
             pltpu.VMEM((n_beams, stations), jnp.float32),
             pltpu.VMEM((n_beams, stations), jnp.float32),
+            pltpu.VMEM((2, ng, 2 * part_beams, stations), jnp.bfloat16),
+            pltpu.VMEM((2, ng, 2 * part_beams, stations), jnp.bfloat16),
+            pltpu.VMEM((nw, 2, 2 * part_beams, width), jnp.float32),
+            pltpu.VMEM((ng - 1, nw, 2, 2 * part_beams, width), jnp.bfloat16),
+            pltpu.VMEM((ng - 1, nw, 2, 2 * part_beams, width), jnp.bfloat16),
             pltpu.VMEM((2, inputs, samples), jnp.bfloat16),
-            pltpu.VMEM((2, inputs, samples), jnp.bfloat16),
+            pltpu.VMEM((nw, 2, inputs, width), jnp.bfloat16),
             pltpu.VMEM((2, rows, inputs), jnp.float32),
             pltpu.VMEM((nt, 2, rows, cols), jnp.bfloat16),
             pltpu.VMEM((nt - 1, 2, rows, cols), jnp.bfloat16),
             pltpu.VMEM((ITERS, ng * nt, 2, rows), jnp.float32),
             pltpu.VMEM((2, inputs), jnp.float32),
             pltpu.VMEM((nf, 2, inputs), jnp.float32),
-            dma((2, nf - 1, nc)),
-            dma((2, nf - 1, nc)),
-            dma((2, ng - 1, nf, nc)),
-            dma((2, ng - 1, nf, nc)),
-            dma((2,)),
+            dma((nf - 1, nc)),
+            dma((nf - 1, nc)),
+            dma((ng - 1, nf, nc)),
+            dma((ng - 1, nf, nc)),
+            dma((nf - 1, nw)),
+            dma((nf - 1, nw)),
+            dma((ng - 1, nw)),
+            dma((ng - 1, nw)),
+            dma,
             dma((nt - 1,)),
             dma((nt - 1,)),
             dma((ITERS, ng * nt - 1)),
             dma((ITERS, ng * nt - 1)),
             dma((nf - 1,)),
             dma((nf - 1,)),
+            dma((8,)),
+            pltpu.VMEM(voltages.shape, jnp.bfloat16),
+            pltpu.VMEM(prior_gains.shape, jnp.float32),
+            pltpu.VMEM((1, stations), jnp.int32),
+            pltpu.VMEM((1, stations), jnp.int32),
+            pltpu.VMEM(station_coords.shape, jnp.float32),
+            pltpu.VMEM(pointing.shape, jnp.int32),
+            pltpu.SMEM(corr_channels.shape, jnp.int32),
+            pltpu.SMEM(beam_channels.shape, jnp.int32),
         ],
         compiler_params=pltpu.CompilerParams(
             collective_id=0, has_side_effects=True, vmem_limit_bytes=48 * 1024 * 1024

time: 154 us -> 156 us (1.013)
  Pallas kernels: 144 us -> 146 us
    pallas_call x1, Pallas kernels: 144 us -> 146 us  [body(): pl.pallas_call(functools.partial(kernel, nf, nt, ng, chunks, nw), out_sha...]
where the time goes in v3:
time: 156 us
  Pallas kernels  146 us (94%)
  local copies, waits for them, and re-layouts  8.86 us (6%)
    pallas_call x1, Pallas kernels, body(): pl.pallas_call(functools.partial(kernel, nf, nt, ng, chunks, nw), out_sha...  146 us
    unnamed x19, local copies, waits for them, and re-layouts  8.86 us

profile of v3, /device:TPU:0, one launch (start us, length us, event | category | flops | bytes accessed | tf_op | source)
XLA Modules:
  0.0 155.8 jit_solution(15895936303089812385)
XLA Ops:
  0.6 0.0 copy-start
  0.6 1.6 %copy-done = bf16[4,2,128,1024]{3,2,1,0:T(8,128)(2,1)S(1)} copy-done((bf16[4,2,128,1024]{3,2,1,0:T(8,128)(2,1)S(1)}, bf16[4,2,128,1024]{3,2,1,0:T(8,128)(2,1)}, u32[]{:S(2)}) %copy-start) | copy-done | bytes 2097176
  2.2 0.0 copy-start.1
  2.2 0.7 copy-done.1
  2.9 0.0 copy-start.2
  2.9 0.7 copy-done.2
  3.6 0.0 copy-start.3
  3.6 0.7 copy-done.3
  4.3 0.0 copy-start.4
  4.3 0.7 copy-done.4
  5.0 0.0 copy-start.5
  5.0 0.7 copy-done.5
  5.7 0.0 copy-start.6
  5.7 0.7 copy-done.6
  6.3 0.0 copy-start.7
  6.3 0.7 copy-done.7
  7.0 146.3 %shard_map.103 = (f32[1,2,512,256]{3,2,1,0:T(8,128)S(1)}, f32[1,2,1024]{2,1,0:T(2,128)S(1)}, bf16[1,2,2,128,1024]{4,3,2,1,0:T(8,128)(2,1)S(1)}) custom-call(bf16[4,2,128,1024]{3,2,1,0:T(8,128)(2,1)S(1)} %copy-done, f32[1,2,1024]{2,1,0:T(2,128)S(1)} %copy-done.1, s32[1,512]{1,0:T(1,128)S(1)} %bitcast.2, s32[1,512]{1,0:T(1,128)S(1)} %bitcast.3, ...), custom_call_target="tpu_custom_call" | custom-call | tf_op jit(solution)/shard_map/pallas_call | solution.py:449
  153.3 1.0 copy.14
  154.2 0.6 copy.15
  154.8 1.0 copy.16
Async XLA Ops:
  0.6 1.6 %copy-start = (bf16[4,2,128,1024]{3,2,1,0:T(8,128)(2,1)S(1)}, bf16[4,2,128,1024]{3,2,1,0:T(8,128)(2,1)}, u32[]{:S(2)}) copy-start(bf16[4,2,128,1024]{3,2,1,0:T(8,128)(2,1)} %refs_0_.1) | copy-start | bytes 6291460
  2.2 0.7 copy-start.1
  2.9 0.7 copy-start.2
  3.6 0.7 copy-start.3
  4.3 0.7 copy-start.4
  5.0 0.7 copy-start.5
  5.7 0.7 copy-start.6
  6.3 0.7 copy-start.7

commit v4 on v3

--- a/solution.py
+++ b/solution.py
@@ -229,7 +229,8 @@
         forward(0, ci)
     own_copy.start()
     pick_beams()
-    for w in range(nw):
+    early = (5 * nw) // 8
+    for w in range(early):
         for k in masks:
             b_copy(k, w).start()
     clear_others()
@@ -273,7 +274,6 @@
         def _():
             stage[i, 0] = real.astype(jnp.bfloat16)
             stage[i, 1] = imag.astype(jnp.bfloat16)
-            vis_copy(i).start()
 
         return carry
 
@@ -316,6 +316,9 @@
         lax.fori_loop(0, rows // strip, product, 0)
         for o in range(len(offsets)):
             update_copy(iteration, o).start()
+        if iteration == ITERS - 1:
+            for i in range(nt - 1):
+                vis_copy(i).start()
         for o in range(len(offsets)):
             update_copy(iteration, o).wait_recv()
         for h in range(ng):
@@ -340,15 +343,9 @@
 
     for k in masks:
         gain_copy(k).start()
-    for i in range(nt - 1):
-        vis_copy(i).wait_recv()
-    own_tile = pl.ds(pl.multiple_of(t * cols, cols), cols)
-    for part in (0, 1):
-        total = gram[part, :, own_tile]
-        for i in range(nt - 1):
-            total = total + landed[i, part].astype(jnp.float32)
-        vis_out[0, part] = total
-
+    for w in range(early, nw):
+        for k in masks:
+            b_copy(k, w).start()
     for k in masks:
         gain_copy(k).wait_recv()
     selected = jnp.zeros_like(z)
@@ -387,6 +384,15 @@
             p_copy(dg, w).start()
         for p in (0, 1):
             mine_beams[w, p] = beamform(p, w, g)
+
+    for i in range(nt - 1):
+        vis_copy(i).wait_recv()
+    own_tile = pl.ds(pl.multiple_of(t * cols, cols), cols)
+    for part in (0, 1):
+        total = gram[part, :, own_tile]
+        for i in range(nt - 1):
+            total = total + landed[i, part].astype(jnp.float32)
+        vis_out[0, part] = total
 
     for w in range(nw):
         lanes = slice(w * width, (w + 1) * width)
@@ -439,7 +445,7 @@
     rows, cols = inputs // ng, inputs // nt
     n_beams = pointing.shape[1]
     part_beams = n_beams // ng
-    nw = 4
+    nw = 8
     width = samples // nw
     step = min(per_input, 32)
     chunks = tuple((part, first, step) for first in range(0, per_input, step) for part in (0, 1))
@@ -500,7 +506,7 @@
             pltpu.SMEM(beam_channels.shape, jnp.int32),
         ],
         compiler_params=pltpu.CompilerParams(
-            collective_id=0, has_side_effects=True, vmem_limit_bytes=48 * 1024 * 1024
+            collective_id=0, has_side_effects=True, vmem_limit_bytes=67043328
         ),
     )(
         voltages,

time: 156 us -> 131 us (0.84)
  Pallas kernels: 146 us -> 126 us
  local copies, waits for them, and re-layouts: 8.86 us -> 3.93 us
    pallas_call x1, Pallas kernels: 146 us -> 126 us  [body(): pl.pallas_call(functools.partial(kernel, nf, nt, ng, chunks, nw), out_sha...]
    unnamed x19 -> x7, local copies, waits for them, and re-layouts: 8.86 us -> 3.93 us
where the time goes in v4:
time: 131 us; the launch traced here: 130 us
  Pallas kernels  126 us (96%)
  local copies, waits for them, and re-layouts  3.93 us (3%)
    pallas_call x1, Pallas kernels, body(): pl.pallas_call(functools.partial(kernel, nf, nt, ng, chunks, nw), out_sha...  126 us
    unnamed x7, local copies, waits for them, and re-layouts  3.93 us

profile of v4, /device:TPU:0, one launch (start us, length us, event | category | flops | bytes accessed | tf_op | source)
XLA Modules:
  0.0 130.4 jit_solution(15652255019442580398)
XLA Ops:
  0.6 125.8 %shard_map.103 = (f32[1,2,512,256]{3,2,1,0:T(8,128)}, f32[1,2,1024]{2,1,0:T(2,128)}, bf16[1,2,2,128,1024]{4,3,2,1,0:T(8,128)(2,1)}) custom-call(bf16[4,2,128,1024]{3,2,1,0:T(8,128)(2,1)} %refs_0_.1, f32[1,2,1024]{2,1,0:T(2,128)} %refs_1_.1, s32[1,512]{1,0:T(1,128)} %bitcast.2, s32[1,512]{1,0:T(1,128)} %bitcast.3, f32[2,512]{1,0:T(2,128)} %refs_4_.1, ...), custom_call_target="tpu_custom_call" | custom-call | tf_op jit(solution)/shard_map/pallas_call | solution.py:455
  126.5 0.0 copy-start.1
  126.5 0.0 copy-start
  126.5 2.4 %copy.14 = f32[1,2,512,256]{3,2,1,0:T(8,128)} copy(f32[1,2,512,256]{3,2,1,0:T(8,128)} %get-tuple-element.6) | data formatting | bytes 2097152
  128.8 0.0 copy-done.1
  128.8 0.6 copy.15
  129.4 0.0 copy-done
  129.4 1.0 copy.16
Async XLA Ops:
  126.5 2.4 %copy-start.1 = (f32[1,2,1024]{2,1,0:T(2,128)S(1)}, f32[1,2,1024]{2,1,0:T(2,128)}, u32[]{:S(2)}) copy-start(f32[1,2,1024]{2,1,0:T(2,128)} %get-tuple-element.7) | copy-start | bytes 24580
  126.5 3.0 %copy-start = (bf16[1,2,2,128,1024]{4,3,2,1,0:T(8,128)(2,1)S(1)}, bf16[1,2,2,128,1024]{4,3,2,1,0:T(8,128)(2,1)}, u32[]{:S(2)}) copy-start(bf16[1,2,2,128,1024]{4,3,2,1,0:T(8,128)(2,1)} %get-tuple-element.8) | copy-start | bytes 3145732
